TPU v7x, 32 devices: a whole 2x2x4 slice. The times are simulated.
32 devices in a mesh: rows: 8 (over y, x, core), cols: 4 (over z).
Axes of the slice: x: 2, y: 2, z: 4, core: 2. Of those that a mesh axis runs over, the one named last changes fastest.
Arguments:
- matrix: float32 [16384, 512], P('rows', 'cols'), may hold values from -48 to 48
- partners: int32 [2, 4], replicated, may hold values from 0 to 3, each once within a row
Outputs:
- rotated: float32 [16384, 512], P('rows', 'cols')
Inputs may be any that keep to these rules, and one draw needn't show every extreme that they name: Each row of partners names every block once.
All inputs are finite; a program needn't handle non-finite values.
Results may differ from a plain program's by a relative error of at most 0.00028.
Values sent between devices are 32-bit elements; how exact they have to be, the bound alone decides.
No kernel may reach another device: no remote copies, remote signals or barrier semaphores. Data moves between devices by JAX's collectives and lax.ppermute only.
A program may use at most 64 MiB of HBM per device.

v0:
```python
import jax
import jax.numpy as jnp
from jax import lax
from jax.sharding import PartitionSpec as P

CYCLE = 3
MATCHED = 2
STEPS = 12
epsilon = 1e-06
highest = lax.Precision.HIGHEST


def from_behind(array, axis, by):
    count = lax.axis_size(axis)
    return lax.ppermute(array, axis, [(i, (i + by) % count) for i in range(count)])


def start_iterate(gram_full):
    order = gram_full.shape[0]
    scale = lax.rsqrt(jnp.diagonal(gram_full) + epsilon)
    normed = gram_full * scale[:, None] * scale[None, :]
    kernel = jnp.eye(order, dtype=jnp.float32) + jnp.triu(normed, 1) - jnp.tril(normed, -1)
    return kernel / jnp.sqrt(jnp.sum(kernel * kernel))


def polar_whole(start):

    def advance(counter, current):
        inner = jnp.dot(current.T, current, precision=highest)
        return 1.5 * current - 0.5 * jnp.dot(current, inner, precision=highest)

    return lax.fori_loop(0, STEPS, advance, start)


def body(matrix, partners):
    current = matrix
    row_count, width = current.shape
    groups = lax.axis_size("cols")
    for meeting in range(CYCLE + MATCHED):
        if meeting < CYCLE:
            other = from_behind(current, "cols", meeting + 1)
        else:
            pieces = current.reshape(groups, row_count // groups, width)
            spread = lax.all_to_all(pieces, "cols", split_axis=0, concat_axis=0, tiled=True)
            chosen = jnp.take(spread, partners[meeting - CYCLE], axis=0)
            other = lax.all_to_all(chosen, "cols", split_axis=0, concat_axis=0, tiled=True).reshape(
                row_count, width
            )
        paired = jnp.concatenate([other, current], axis=1)
        local_gram = jnp.einsum("ra,rb->ab", paired, paired, precision=highest)
        gram_sum = lax.psum(local_gram, "rows")
        start = start_iterate(gram_sum)
        rotation = polar_whole(start)
        current = jnp.dot(paired, rotation[:, width:], precision=highest)
    return current


def solution(mesh):
    placed = (P("rows", "cols"), P())
    return jax.shard_map(
        body, mesh=mesh, in_specs=placed, out_specs=P("rows", "cols"), check_vma=False
    )
```

profile of v0, /device:TPU:0, one launch (start us, length us, event | category | flops | bytes accessed | tf_op | source)
XLA Modules:
  0.0 627.4 jit_solution(489708078406153949)
XLA Ops:
  9.6 25.5 %collective-permute-done = f32[2048,128]{1,0:T(8,128)S(1)} collective-permute-done((f32[2048,128]{1,0:T(8,128)}, f32[2048,128]{1,0:T(8,128)S(1)}, u32[]{:S(2)}, u32[]{:S(2)}) %collective-permute-start) | collective-permute-done | bytes 1048608 | tf_op jit(solution)/shard_map/ppermute | solution.py:15
  35.2 4.3 fusion.42
  39.7 53.3 %all-reduce.6.cloned.1.call-done = f32[256,256]{1,0:T(8,128)} async-done(((f32[256,256]{1,0:T(8,128)}), f32[256,256]{1,0:T(8,128)}) %all-reduce.6.cloned.1.call-update) | async-done | bytes 262160 | tf_op jit(solution)/shard_map/psum | solution.py:51
  99.2 12.7 %while.50 = (s32[]{:T(128)}, f32[256,256]{0,1:T(8,128)S(1)}, s32[]{:T(128)}) while((s32[]{:T(128)}, f32[256,256]{0,1:T(8,128)S(1)}, s32[]{:T(128)}) %tuple.85), condition=%wide.region_3.4_spmd, body=%wide.region_2.3_spmd.sunk | while | flops 402849792 | bytes 1835053 | solution.py:32
  116.7 45.1 %collective-permute-done.1 = f32[2048,128]{0,1:T(8,128)S(1)} collective-permute-done((f32[2048,128]{0,1:T(8,128)S(1)}, f32[2048,128]{0,1:T(8,128)S(1)}, u32[]{:S(2)}, u32[]{:S(2)}) %collective-permute-start.1) | collective-permute-done | bytes 1048608 | tf_op jit(solution)/shard_map/ppermute | solution.py:15
  164.9 52.8 %all-reduce.8.cloned.1.call-done = f32[256,256]{1,0:T(8,128)} async-done(((f32[256,256]{1,0:T(8,128)}), f32[256,256]{1,0:T(8,128)}) %all-reduce.8.cloned.1.call-update) | async-done | bytes 262160 | tf_op jit(solution)/shard_map/psum | solution.py:51
  224.0 12.8 %while.51 = (s32[]{:T(128)}, f32[256,256]{0,1:T(8,128)S(1)}, s32[]{:T(128)}) while((s32[]{:T(128)}, f32[256,256]{0,1:T(8,128)S(1)}, s32[]{:T(128)}) %tuple.88), condition=%wide.region_7.8_spmd, body=%wide.region_6.7_spmd.sunk | while | flops 402849792 | bytes 1835053 | solution.py:32
  241.4 21.6 %collective-permute-done.2 = f32[2048,128]{0,1:T(8,128)S(1)} collective-permute-done((f32[2048,128]{0,1:T(8,128)S(1)}, f32[2048,128]{0,1:T(8,128)S(1)}, u32[]{:S(2)}, u32[]{:S(2)}) %collective-permute-start.2) | collective-permute-done | bytes 1048608 | tf_op jit(solution)/shard_map/ppermute | solution.py:15
  265.6 54.3 %all-reduce.10.cloned.1.call-done = f32[256,256]{1,0:T(8,128)} async-done(((f32[256,256]{1,0:T(8,128)}), f32[256,256]{1,0:T(8,128)}) %all-reduce.10.cloned.1.call-update) | async-done | bytes 262160 | tf_op jit(solution)/shard_map/psum | solution.py:51
  326.2 12.7 %while.52 = (s32[]{:T(128)}, f32[256,256]{0,1:T(8,128)S(1)}, s32[]{:T(128)}) while((s32[]{:T(128)}, f32[256,256]{0,1:T(8,128)S(1)}, s32[]{:T(128)}) %tuple.91), condition=%wide.region_11.12_spmd, body=%wide.region_10.11_spmd.sunk | while | flops 402849792 | bytes 1835053 | solution.py:32
  338.9 4.5 fusion.14
  343.5 4.6 all-to-all-start
  348.1 24.9 %all-to-all-done = f32[4,512,128]{2,1,0:T(8,128)S(1)} async-done(((f32[4,512,128]{2,1,0:T(8,128)}), f32[4,512,128]{2,1,0:T(8,128)S(1)}, u32[]{:S(2)}, u32[]{:S(2)}) %all-to-all-start) | async-done | bytes 1048608 | tf_op jit(solution)/shard_map/all_to_all | solution.py:44
  373.8 27.9 %all_to_all.20 = f32[4,512,128]{2,1,0:T(8,128)S(1)} all-to-all(f32[4,512,128]{2,1,0:T(8,128)S(1)} %broadcast_select_fusion.1), channel_id=1, replica_groups=mesh['rows'=8,'cols'=4] {'cols'}, dimensions={0} | all-to-all | bytes 2097152 | tf_op jit(solution)/shard_map/all_to_all | solution.py:46
  401.7 5.9 fusion.13
  407.6 51.5 %all-reduce.12.cloned.1.call-done = f32[256,256]{1,0:T(8,128)} async-done(((f32[256,256]{1,0:T(8,128)}), f32[256,256]{1,0:T(8,128)}) %all-reduce.12.cloned.1.call-update) | async-done | bytes 262160 | tf_op jit(solution)/shard_map/psum | solution.py:51
  465.3 12.7 %while.53 = (s32[]{:T(128)}, f32[256,256]{0,1:T(8,128)S(1)}, s32[]{:T(128)}) while((s32[]{:T(128)}, f32[256,256]{0,1:T(8,128)S(1)}, s32[]{:T(128)}) %tuple.94), condition=%wide.region_15.17_spmd, body=%wide.region_14.16_spmd.sunk | while | flops 402849792 | bytes 1835053 | solution.py:32
  478.1 4.0 fusion.12
  482.1 4.6 all-to-all-start.2
  486.7 24.9 %all-to-all-done.2 = f32[4,512,128]{2,1,0:T(8,128)S(1)} async-done(((f32[4,512,128]{2,1,0:T(8,128)}), f32[4,512,128]{2,1,0:T(8,128)S(1)}, u32[]{:S(2)}, u32[]{:S(2)}) %all-to-all-start.2) | async-done | bytes 1048608 | tf_op jit(solution)/shard_map/all_to_all | solution.py:44
  512.4 27.9 %all_to_all.21 = f32[4,512,128]{2,1,0:T(8,128)S(1)} all-to-all(f32[4,512,128]{2,1,0:T(8,128)S(1)} %broadcast_select_fusion), channel_id=1, replica_groups=mesh['rows'=8,'cols'=4] {'cols'}, dimensions={0} | all-to-all | bytes 2097152 | tf_op jit(solution)/shard_map/all_to_all | solution.py:46
  540.3 5.9 fusion.11
  546.2 51.5 %all-reduce.14.cloned.1.call-done = f32[256,256]{1,0:T(8,128)} async-done(((f32[256,256]{1,0:T(8,128)}), f32[256,256]{1,0:T(8,128)}) %all-reduce.14.cloned.1.call-update) | async-done | bytes 262160 | tf_op jit(solution)/shard_map/psum | solution.py:51
  603.9 12.8 %while.54 = (s32[]{:T(128)}, f32[256,256]{0,1:T(8,128)S(1)}, s32[]{:T(128)}) while((s32[]{:T(128)}, f32[256,256]{0,1:T(8,128)S(1)}, s32[]{:T(128)}) %tuple.97), condition=%wide.region_19.21_spmd, body=%wide.region_18.20_spmd.sunk | while | flops 402849792 | bytes 1835053 | solution.py:32
  (238 shorter events, 113.1 us)
Async XLA Ops:
  6.5 28.6 %copy-start = (f32[2048,128]{1,0:T(8,128)S(1)}, f32[2048,128]{1,0:T(8,128)}, u32[]{:S(2)}) copy-start(f32[2048,128]{1,0:T(8,128)} %param.14) | copy-start | bytes 3145732
  6.5 86.4 %all-reduce.6.cloned.1.call-start = ((), (), s32[]{:S(2)}) async-start(), calls=%async_computation.4 | async-start | bytes 524288 | tf_op jit(solution)/shard_map/psum | solution.py:51
  6.5 28.5 %collective-permute-start = (f32[2048,128]{1,0:T(8,128)}, f32[2048,128]{1,0:T(8,128)S(1)}, u32[]{:S(2)}, u32[]{:S(2)}) collective-permute-start(f32[2048,128]{1,0:T(8,128)} %param.14), channel_id=1, source_target_pairs={{0,1},{1,2},{2,3},{3,0},{4,5},{5,6},{6,7},{7,4},{8,9},{9,10},{10,1... | collective-permute-start | bytes 3145736 | tf_op jit(solution)/shard_map/ppermute | solution.py:15
  39.6 178.1 %all-reduce.8.cloned.1.call-start = ((), (), s32[]{:S(2)}) async-start(), calls=%async_computation.5 | async-start | bytes 524288 | tf_op jit(solution)/shard_map/psum | solution.py:51
  114.2 47.6 %collective-permute-start.1 = (f32[2048,128]{0,1:T(8,128)S(1)}, f32[2048,128]{0,1:T(8,128)S(1)}, u32[]{:S(2)}, u32[]{:S(2)}) collective-permute-start(f32[2048,128]{0,1:T(8,128)S(1)} %fusion.27), channel_id=1, source_target_pairs={{0,2},{1,3},{2,0},{3,1},{4,6},{5,7},{6,4},{7,5},{8,10},{9,11},{10,... | collective-permute-start | bytes 3145736 | tf_op jit(solution)/shard_map/ppermute | solution.py:15
  164.4 155.6 %all-reduce.10.cloned.1.call-start = ((), (), s32[]{:S(2)}) async-start(), calls=%async_computation.6 | async-start | bytes 524288 | tf_op jit(solution)/shard_map/psum | solution.py:51
  238.0 25.0 %collective-permute-start.2 = (f32[2048,128]{0,1:T(8,128)S(1)}, f32[2048,128]{0,1:T(8,128)S(1)}, u32[]{:S(2)}, u32[]{:S(2)}) collective-permute-start(f32[2048,128]{0,1:T(8,128)S(1)} %fusion.16), channel_id=1, source_target_pairs={{0,3},{1,0},{2,1},{3,2},{4,7},{5,4},{6,5},{7,6},{8,11},{9,8},{10,9... | collective-permute-start | bytes 3145736 | tf_op jit(solution)/shard_map/ppermute | solution.py:15
  338.9 9.2 %copy-start.1 = (s32[2,4]{1,0:T(2,128)S(1)}, s32[2,4]{1,0:T(2,128)}, u32[]{:S(2)}) copy-start(s32[2,4]{1,0:T(2,128)} %param.15) | copy-start | bytes 100
  343.5 29.5 %all-to-all-start = ((f32[4,512,128]{2,1,0:T(8,128)}), f32[4,512,128]{2,1,0:T(8,128)S(1)}, u32[]{:S(2)}, u32[]{:S(2)}) async-start(f32[4,512,128]{2,1,0:T(8,128)} %bitcast.8), calls=%async_computation | async-start | bytes 2097152 | tf_op jit(solution)/shard_map/all_to_all | solution.py:44
  348.1 111.0 %all-reduce.12.cloned.1.call-start = ((), (), s32[]{:S(2)}) async-start(), calls=%async_computation.7 | async-start | bytes 524288 | tf_op jit(solution)/shard_map/psum | solution.py:51
  482.1 29.5 %all-to-all-start.2 = ((f32[4,512,128]{2,1,0:T(8,128)}), f32[4,512,128]{2,1,0:T(8,128)S(1)}, u32[]{:S(2)}, u32[]{:S(2)}) async-start(f32[4,512,128]{2,1,0:T(8,128)} %bitcast.10), calls=%async_computation.2 | async-start | bytes 2097152 | tf_op jit(solution)/shard_map/all_to_all | solution.py:44
  486.7 111.0 %all-reduce.14.cloned.1.call-start = ((), (), s32[]{:S(2)}) async-start(), calls=%async_computation.8 | async-start | bytes 524288 | tf_op jit(solution)/shard_map/psum | solution.py:51
Sparse Core Ops, SparseCore 0:
  39.7 53.1 all-reduce.5
  164.5 53.1 all-reduce.7
  265.7 54.1 all-reduce.9
  407.7 51.3 all-reduce.11
  546.3 51.3 all-reduce.13
where the time goes:
time: 636 us; the launch traced here: 627 us
  waiting for transfers between devices  405 us (64%)
  matrix products  97.6 us (15%)
  blocking collectives  55.8 us (9%)
  starting transfers between devices  18.7 us (3%)
  between operations  17 us (3%)
  local copies, waits for them, and re-layouts  16 us (3%)
  other arithmetic  14.5 us (2%)
    psum x5, waiting for transfers between devices, body(): gram_sum = lax.psum(local_gram, 'rows')  263 us
    ppermute x3, waiting for transfers between devices, from_behind(): lax.ppermute(array, axis, [(i, (i + by) % count) for i in range(count)])  92.1 us
    all_to_all x2, blocking collectives, body(): lax.all_to_all(chosen, 'cols', split_axis=0, concat_axis=0, tiled=True)  55.8 us
    all_to_all x2, waiting for transfers between devices, body(): lax.all_to_all(pieces, 'cols', split_axis=0, concat_axis=0, tiled=True)  49.8 us
    dot_general x60, matrix products, advance(): return 1.5 * current - 0.5 * jnp.dot(current, inner, precision=highest)  35.9 us
    dot_general x60, matrix products, advance(): inner = jnp.dot(current.T, current, precision=highest)  24.4 us
    dot_general x5, matrix products, body(): local_gram = jnp.einsum('ra,rb->ab', paired, paired, precision=highest)  21.2 us
    dot_general x5, matrix products, body(): current = jnp.dot(paired, rotation[:, width:], precision=highest)  16.2 us
  transfers between devices with their start and end apart: 10, of which 10 were waited for; matrix products, arithmetic and copies ran while one was open for 0% of the time, Pallas kernels for 0%

commit v1 on v0

--- a/solution.py
+++ b/solution.py
@@ -48,7 +48,7 @@
             )
         paired = jnp.concatenate([other, current], axis=1)
         local_gram = jnp.einsum("ra,rb->ab", paired, paired, precision=highest)
-        gram_sum = lax.psum(local_gram, "rows")
+        gram_sum = jnp.sum(lax.all_gather(local_gram, "rows"), axis=0)
         start = start_iterate(gram_sum)
         rotation = polar_whole(start)
         current = jnp.dot(paired, rotation[:, width:], precision=highest)

time: 636 us -> 512 us (0.81)
  waiting for transfers between devices: 405 us -> 282 us
    psum x5 -> x0, waiting for transfers between devices: 263 us -> none  [body(): gram_sum = lax.psum(local_gram, 'rows')]
    all_gather x0 -> x5, waiting for transfers between devices: none -> 136 us  [body(): gram_sum = jnp.sum(lax.all_gather(local_gram, 'rows'), axis=0)]
    reduce_sum x0 -> x5, other arithmetic: none -> 8.8 us  [body(): gram_sum = jnp.sum(lax.all_gather(local_gram, 'rows'), axis=0)]
where the time goes in v1:
time: 512 us; the launch traced here: 505 us
  waiting for transfers between devices  282 us (55%)
  matrix products  99 us (19%)
  blocking collectives  55.8 us (11%)
  starting transfers between devices  18.6 us (4%)
  between operations  17 us (3%)
  local copies, waits for them, and re-layouts  15.9 us (3%)
  other arithmetic  13.7 us (3%)
    all_gather x5, waiting for transfers between devices, body(): gram_sum = jnp.sum(lax.all_gather(local_gram, 'rows'), axis=0)  136 us
    ppermute x3, waiting for transfers between devices, from_behind(): lax.ppermute(array, axis, [(i, (i + by) % count) for i in range(count)])  94.5 us
    all_to_all x2, blocking collectives, body(): lax.all_to_all(chosen, 'cols', split_axis=0, concat_axis=0, tiled=True)  55.8 us
    all_to_all x2, waiting for transfers between devices, body(): lax.all_to_all(pieces, 'cols', split_axis=0, concat_axis=0, tiled=True)  52.2 us
    dot_general x60, matrix products, advance(): return 1.5 * current - 0.5 * jnp.dot(current, inner, precision=highest)  35.9 us
    dot_general x60, matrix products, advance(): inner = jnp.dot(current.T, current, precision=highest)  24.4 us
    dot_general x5, matrix products, body(): local_gram = jnp.einsum('ra,rb->ab', paired, paired, precision=highest)  21.3 us
    dot_general x5, matrix products, body(): current = jnp.dot(paired, rotation[:, width:], precision=highest)  17.4 us
  transfers between devices with their start and end apart: 10, of which 10 were waited for; matrix products, arithmetic and copies ran while one was open for 0% of the time, Pallas kernels for 0%

profile of v1, /device:TPU:0, one launch (start us, length us, event | category | flops | bytes accessed | tf_op | source)
XLA Modules:
  0.0 504.6 jit_solution(9530485871418048939)
XLA Ops:
  9.6 25.5 %collective-permute-done = f32[2048,128]{1,0:T(8,128)S(1)} collective-permute-done((f32[2048,128]{1,0:T(8,128)}, f32[2048,128]{1,0:T(8,128)S(1)}, u32[]{:S(2)}, u32[]{:S(2)}) %collective-permute-start) | collective-permute-done | bytes 1048608 | tf_op jit(solution)/shard_map/ppermute | solution.py:15
  35.2 4.3 fusion.42
  39.7 27.2 %all-gather.11.cloned.1.call-done = f32[2048,256]{1,0:T(8,128)} async-done(((f32[256,256]{1,0:T(8,128)}), f32[2048,256]{1,0:T(8,128)}) %all-gather.11.cloned.1.call-update) | async-done | bytes 2097168 | tf_op jit(solution)/shard_map/all_gather | solution.py:51
  72.7 12.7 %while.50 = (s32[]{:T(128)}, f32[256,256]{0,1:T(8,128)S(1)}, s32[]{:T(128)}) while((s32[]{:T(128)}, f32[256,256]{0,1:T(8,128)S(1)}, s32[]{:T(128)}) %tuple.85), condition=%wide.region_3.4_spmd, body=%wide.region_2.3_spmd.sunk | while | flops 402849792 | bytes 1835053 | solution.py:32
  90.2 46.3 %collective-permute-done.1 = f32[2048,128]{0,1:T(8,128)S(1)} collective-permute-done((f32[2048,128]{0,1:T(8,128)S(1)}, f32[2048,128]{0,1:T(8,128)S(1)}, u32[]{:S(2)}, u32[]{:S(2)}) %collective-permute-start.1) | collective-permute-done | bytes 1048608 | tf_op jit(solution)/shard_map/ppermute | solution.py:15
  140.6 27.4 %all-gather.13.cloned.1.call-done = f32[2048,256]{1,0:T(8,128)} async-done(((f32[256,256]{1,0:T(8,128)}), f32[2048,256]{1,0:T(8,128)}) %all-gather.13.cloned.1.call-update) | async-done | bytes 2097168 | tf_op jit(solution)/shard_map/all_gather | solution.py:51
  173.8 12.7 %while.51 = (s32[]{:T(128)}, f32[256,256]{0,1:T(8,128)S(1)}, s32[]{:T(128)}) while((s32[]{:T(128)}, f32[256,256]{0,1:T(8,128)S(1)}, s32[]{:T(128)}) %tuple.88), condition=%wide.region_7.8_spmd, body=%wide.region_6.7_spmd.sunk | while | flops 402849792 | bytes 1835053 | solution.py:32
  192.5 22.8 %collective-permute-done.2 = f32[2048,128]{0,1:T(8,128)S(1)} collective-permute-done((f32[2048,128]{0,1:T(8,128)S(1)}, f32[2048,128]{0,1:T(8,128)S(1)}, u32[]{:S(2)}, u32[]{:S(2)}) %collective-permute-start.2) | collective-permute-done | bytes 1048608 | tf_op jit(solution)/shard_map/ppermute | solution.py:15
  217.9 28.9 %all-gather.15.cloned.1.call-done = f32[2048,256]{1,0:T(8,128)} async-done(((f32[256,256]{1,0:T(8,128)}), f32[2048,256]{1,0:T(8,128)}) %all-gather.15.cloned.1.call-update) | async-done | bytes 2097168 | tf_op jit(solution)/shard_map/all_gather | solution.py:51
  252.6 12.8 %while.52 = (s32[]{:T(128)}, f32[256,256]{0,1:T(8,128)S(1)}, s32[]{:T(128)}) while((s32[]{:T(128)}, f32[256,256]{0,1:T(8,128)S(1)}, s32[]{:T(128)}) %tuple.91), condition=%wide.region_11.12_spmd, body=%wide.region_10.11_spmd.sunk | while | flops 402849792 | bytes 1835053 | solution.py:32
  265.4 4.5 fusion.14
  269.9 4.6 all-to-all-start
  274.5 26.1 %all-to-all-done = f32[4,512,128]{2,1,0:T(8,128)S(1)} async-done(((f32[4,512,128]{2,1,0:T(8,128)}), f32[4,512,128]{2,1,0:T(8,128)S(1)}, u32[]{:S(2)}, u32[]{:S(2)}) %all-to-all-start) | async-done | bytes 1048608 | tf_op jit(solution)/shard_map/all_to_all | solution.py:44
  301.4 27.9 %all_to_all.20 = f32[4,512,128]{2,1,0:T(8,128)S(1)} all-to-all(f32[4,512,128]{2,1,0:T(8,128)S(1)} %broadcast_select_fusion.1), channel_id=1, replica_groups=mesh['rows'=8,'cols'=4] {'cols'}, dimensions={0} | all-to-all | bytes 2097152 | tf_op jit(solution)/shard_map/all_to_all | solution.py:46
  329.3 5.9 %fusion.13 = f32[256,256]{1,0:T(8,128)} fusion(f32[2048,128]{1,0:T(8,128)} %fusion.14, f32[2048,128]{1,0:T(8,128)S(1)} %bitcast.116), kind=kOutput, calls=%fused_computation.29 | convolution fusion | flops 1611137024 | bytes 2359296 | tf_op jit(solution)/shard_map/ra,rb->ab/dot_general | solution.py:50
  335.3 26.0 %all-gather.17.cloned.1.call-done = f32[2048,256]{1,0:T(8,128)} async-done(((f32[256,256]{1,0:T(8,128)}), f32[2048,256]{1,0:T(8,128)}) %all-gather.17.cloned.1.call-update) | async-done | bytes 2097168 | tf_op jit(solution)/shard_map/all_gather | solution.py:51
  367.1 12.8 %while.53 = (s32[]{:T(128)}, f32[256,256]{0,1:T(8,128)S(1)}, s32[]{:T(128)}) while((s32[]{:T(128)}, f32[256,256]{0,1:T(8,128)S(1)}, s32[]{:T(128)}) %tuple.94), condition=%wide.region_15.17_spmd, body=%wide.region_14.16_spmd.sunk | while | flops 402849792 | bytes 1835053 | solution.py:32
  379.8 4.0 fusion.12
  383.8 4.6 all-to-all-start.2
  388.5 26.1 %all-to-all-done.2 = f32[4,512,128]{2,1,0:T(8,128)S(1)} async-done(((f32[4,512,128]{2,1,0:T(8,128)}), f32[4,512,128]{2,1,0:T(8,128)S(1)}, u32[]{:S(2)}, u32[]{:S(2)}) %all-to-all-start.2) | async-done | bytes 1048608 | tf_op jit(solution)/shard_map/all_to_all | solution.py:44
  415.3 27.9 %all_to_all.21 = f32[4,512,128]{2,1,0:T(8,128)S(1)} all-to-all(f32[4,512,128]{2,1,0:T(8,128)S(1)} %broadcast_select_fusion), channel_id=1, replica_groups=mesh['rows'=8,'cols'=4] {'cols'}, dimensions={0} | all-to-all | bytes 2097152 | tf_op jit(solution)/shard_map/all_to_all | solution.py:46
  443.3 5.9 %fusion.11 = f32[256,256]{1,0:T(8,128)} fusion(f32[2048,128]{1,0:T(8,128)} %fusion.12, f32[2048,128]{1,0:T(8,128)S(1)} %bitcast.114), kind=kOutput, calls=%fused_computation.27 | convolution fusion | flops 1611137024 | bytes 2359296 | tf_op jit(solution)/shard_map/ra,rb->ab/dot_general | solution.py:50
  449.2 26.1 %all-gather.19.cloned.1.call-done = f32[2048,256]{1,0:T(8,128)} async-done(((f32[256,256]{1,0:T(8,128)}), f32[2048,256]{1,0:T(8,128)}) %all-gather.19.cloned.1.call-update) | async-done | bytes 2097168 | tf_op jit(solution)/shard_map/all_gather | solution.py:51
  481.1 12.8 %while.54 = (s32[]{:T(128)}, f32[256,256]{0,1:T(8,128)S(1)}, s32[]{:T(128)}) while((s32[]{:T(128)}, f32[256,256]{0,1:T(8,128)S(1)}, s32[]{:T(128)}) %tuple.97), condition=%wide.region_19.21_spmd, body=%wide.region_18.20_spmd.sunk | while | flops 402849792 | bytes 1835053 | solution.py:32
  (245 shorter events, 113.4 us)
Async XLA Ops:
  6.5 28.6 %copy-start.1 = (f32[2048,128]{1,0:T(8,128)S(1)}, f32[2048,128]{1,0:T(8,128)}, u32[]{:S(2)}) copy-start(f32[2048,128]{1,0:T(8,128)} %param.14) | copy-start | bytes 3145732
  6.5 60.3 %all-gather.11.cloned.1.call-start = ((), (), s32[]{:S(2)}) async-start(), calls=%async_computation.4 | async-start | bytes 2359296 | tf_op jit(solution)/shard_map/all_gather | solution.py:51
  6.5 28.5 %collective-permute-start = (f32[2048,128]{1,0:T(8,128)}, f32[2048,128]{1,0:T(8,128)S(1)}, u32[]{:S(2)}, u32[]{:S(2)}) collective-permute-start(f32[2048,128]{1,0:T(8,128)} %param.14), channel_id=1, source_target_pairs={{0,1},{1,2},{2,3},{3,0},{4,5},{5,6},{6,7},{7,4},{8,9},{9,10},{10,1... | collective-permute-start | bytes 3145736 | tf_op jit(solution)/shard_map/ppermute | solution.py:15
  39.6 128.4 %all-gather.13.cloned.1.call-start = ((), (), s32[]{:S(2)}) async-start(), calls=%async_computation.5 | async-start | bytes 2359296 | tf_op jit(solution)/shard_map/all_gather | solution.py:51
  87.8 48.7 %collective-permute-start.1 = (f32[2048,128]{0,1:T(8,128)S(1)}, f32[2048,128]{0,1:T(8,128)S(1)}, u32[]{:S(2)}, u32[]{:S(2)}) collective-permute-start(f32[2048,128]{0,1:T(8,128)S(1)} %fusion.27), channel_id=1, source_target_pairs={{0,2},{1,3},{2,0},{3,1},{4,6},{5,7},{6,4},{7,5},{8,10},{9,11},{10,... | collective-permute-start | bytes 3145736 | tf_op jit(solution)/shard_map/ppermute | solution.py:15
  136.5 1.0 copy-start
  140.1 106.6 %all-gather.15.cloned.1.call-start = ((), (), s32[]{:S(2)}) async-start(), calls=%async_computation.6 | async-start | bytes 2359296 | tf_op jit(solution)/shard_map/all_gather | solution.py:51
  189.1 26.2 %collective-permute-start.2 = (f32[2048,128]{0,1:T(8,128)S(1)}, f32[2048,128]{0,1:T(8,128)S(1)}, u32[]{:S(2)}, u32[]{:S(2)}) collective-permute-start(f32[2048,128]{0,1:T(8,128)S(1)} %fusion.16), channel_id=1, source_target_pairs={{0,3},{1,0},{2,1},{3,2},{4,7},{5,4},{6,5},{7,6},{8,11},{9,8},{10,9... | collective-permute-start | bytes 3145736 | tf_op jit(solution)/shard_map/ppermute | solution.py:15
  265.4 9.1 %copy-start.2 = (s32[2,4]{1,0:T(2,128)S(1)}, s32[2,4]{1,0:T(2,128)}, u32[]{:S(2)}) copy-start(s32[2,4]{1,0:T(2,128)} %param.15) | copy-start | bytes 100
  269.9 30.7 %all-to-all-start = ((f32[4,512,128]{2,1,0:T(8,128)}), f32[4,512,128]{2,1,0:T(8,128)S(1)}, u32[]{:S(2)}, u32[]{:S(2)}) async-start(f32[4,512,128]{2,1,0:T(8,128)} %bitcast.11), calls=%async_computation | async-start | bytes 2097152 | tf_op jit(solution)/shard_map/all_to_all | solution.py:44
  274.5 86.8 %all-gather.17.cloned.1.call-start = ((), (), s32[]{:S(2)}) async-start(), calls=%async_computation.7 | async-start | bytes 2359296 | tf_op jit(solution)/shard_map/all_gather | solution.py:51
  383.8 30.7 %all-to-all-start.2 = ((f32[4,512,128]{2,1,0:T(8,128)}), f32[4,512,128]{2,1,0:T(8,128)S(1)}, u32[]{:S(2)}, u32[]{:S(2)}) async-start(f32[4,512,128]{2,1,0:T(8,128)} %bitcast.14), calls=%async_computation.2 | async-start | bytes 2097152 | tf_op jit(solution)/shard_map/all_to_all | solution.py:44
  388.4 86.8 %all-gather.19.cloned.1.call-start = ((), (), s32[]{:S(2)}) async-start(), calls=%async_computation.8 | async-start | bytes 2359296 | tf_op jit(solution)/shard_map/all_gather | solution.py:51
Sparse Core Ops, SparseCore 0:
  39.7 27.0 all-gather.10
  140.2 27.7 all-gather.12
  218.0 28.7 all-gather.14
  335.4 25.8 all-gather.16
  449.3 25.8 all-gather.18
